TPU v7x, 128 devices: a whole 4x4x4 slice. The times are simulated.
128 devices in a mesh: layer: 16 (over y, z_hi, core), feat: 8 (over x, z_lo).
Axes of the slice: x: 4, y: 4, z: 4 (z_hi: 2, z_lo: 2; z = z_hi * 2 + z_lo), core: 2. Of those that a mesh axis runs over, the one named last changes fastest.
Arguments:
- tokens_in: bfloat16 [512, 4096], P('feat', 'layer'), may hold values from -6 to 6
- targets: bfloat16 [512, 4096], P('feat', 'layer'), may hold values from -6 to 6
- enc_weight: bfloat16 [2048, 131072], P(None, ('layer', 'feat')), may hold values from -0.125 to 0.125
- enc_bias: float32 [131072], P(('layer', 'feat')), may hold values from -1 to 0.5
- dec_weight: bfloat16 [2, 131072, 2048], P(None, ('layer', 'feat')), may hold values from -0.0234375 to 0.0234375
Outputs:
- recon_error: float32 [512, 4096], P('feat', 'layer')
- mean_square: float32 [], replicated
- enc_grad: bfloat16 [2048, 131072], P(None, ('layer', 'feat'))
- bias_grad: float32 [131072], P(('layer', 'feat'))
- dec_grad: bfloat16 [2, 131072, 2048], P(None, ('layer', 'feat'))
All inputs are finite; a program needn't handle non-finite values.
Results may differ from a plain program's by a relative error of at most 0.02.
Values may be sent and summed in bfloat16 or wider, within the bound.
A program may use at most 128 MiB of HBM per device.

v0:
```python
import jax
import jax.numpy as jnp
from jax import lax
from jax.sharding import PartitionSpec as P

D = 2048
LAYERS = 2
TOK = 512
loss_scale = 64.0


def swapped(value, axis, stride):
    mask = 2**stride
    pairs = [(source, source ^ mask) for source in range(lax.axis_size(axis))]
    return lax.ppermute(value, axis, pairs)


def arrange_group(gathered, which_group, feat_count, sub_count):
    row_count = gathered.shape[1]
    col_count = gathered.shape[2]
    blocks = gathered.reshape(gathered.shape[0] // feat_count, feat_count, row_count, col_count)
    chosen = lax.dynamic_slice_in_dim(blocks, which_group * sub_count, sub_count, 0)
    return jnp.transpose(chosen, (1, 2, 0, 3)).reshape(
        feat_count * row_count, sub_count * col_count
    )


def order_pair(current, partner, member, bit_level, axis_dim):
    lower_first = member >> bit_level & 1 == 0
    leading = jnp.where(lower_first, current, partner)
    trailing = jnp.where(lower_first, partner, current)
    return jnp.concatenate([leading, trailing], axis_dim)


def on_device(tokens_in, targets, enc_weight, enc_bias, dec_weight):
    sub_count = lax.axis_size("layer") // LAYERS
    position = lax.axis_index("layer")
    layer_group = position // sub_count
    member = position % sub_count
    feat_count = lax.axis_size("feat")
    row_count = tokens_in.shape[0]
    col_count = tokens_in.shape[1]
    bit_count = sub_count.bit_length() - 1
    joined = tokens_in
    for bit_level in range(bit_count):
        partner = swapped(joined, "layer", bit_level)
        joined = order_pair(joined, partner, member, bit_level, 1)
    inputs = lax.all_gather(joined, "feat", axis=0, tiled=True)
    pre_act = jnp.dot(inputs, enc_weight, preferred_element_type=jnp.float32) + enc_bias
    features = jnp.maximum(pre_act, 0.0).astype(jnp.bfloat16)
    partial_value = jnp.einsum(
        "tf,kfd->tkd", features, dec_weight, preferred_element_type=jnp.float32
    )
    summed = lax.psum(partial_value.astype(jnp.bfloat16), "feat").astype(jnp.float32)
    summed_rows = lax.dynamic_slice_in_dim(summed, lax.axis_index("feat") * row_count, row_count, 0)
    gathered = lax.all_gather(
        summed_rows[None].astype(jnp.bfloat16), "layer", axis=0, tiled=True
    ).astype(jnp.float32)
    columns = lax.dynamic_slice_in_dim(gathered, member * col_count, col_count, 3)
    own_part = jnp.sum(
        lax.dynamic_slice_in_dim(columns, layer_group * sub_count, sub_count, 0)[:, :, 0, :], 0
    )
    prev_part = jnp.sum(
        lax.dynamic_slice_in_dim(
            columns, jnp.maximum(layer_group - 1, 0) * sub_count, sub_count, 0
        )[:, :, 1, :],
        0,
    )
    rebuilt = own_part + jnp.where(layer_group > 0, prev_part, 0.0)
    recon_error = rebuilt - targets.astype(jnp.float32)
    squares = lax.psum(jnp.sum(recon_error * recon_error), ("layer", "feat"))
    mean_square = squares / (LAYERS * TOK * D)
    scaled = (loss_scale / TOK * recon_error).astype(jnp.bfloat16)
    gathered = lax.all_gather(scaled[None], ("layer", "feat"), axis=0, tiled=True)
    own_grad = arrange_group(gathered, layer_group, feat_count, sub_count)
    next_index = jnp.minimum(layer_group + 1, LAYERS - 1)
    next_grad = arrange_group(gathered, next_index, feat_count, sub_count)
    next_grad = jnp.where(layer_group + 1 < LAYERS, next_grad, jnp.zeros_like(next_grad))
    recon_grads = jnp.stack([own_grad, next_grad], 0)
    feature_grad = jnp.einsum(
        "ktd,kfd->tf", recon_grads, dec_weight, preferred_element_type=jnp.float32
    )
    preact_grad = jnp.where(pre_act > 0.0, feature_grad, 0.0).astype(jnp.bfloat16)
    dec_grad = jnp.einsum(
        "tf,ktd->kfd", features, recon_grads, preferred_element_type=jnp.float32
    ).astype(jnp.bfloat16)
    enc_grad = lax.dot_general(
        inputs, preact_grad, (((0,), (0,)), ((), ())), preferred_element_type=jnp.float32
    ).astype(jnp.bfloat16)
    bias_grad = jnp.sum(preact_grad.astype(jnp.float32), 0)
    return (recon_error, mean_square, enc_grad, bias_grad, dec_grad)


def solution(mesh):
    placed = (
        P("feat", "layer"),
        P("feat", "layer"),
        P(None, ("layer", "feat")),
        P(("layer", "feat")),
        P(None, ("layer", "feat"), None),
    )
    return jax.shard_map(
        on_device,
        mesh=mesh,
        in_specs=placed,
        out_specs=(
            P("feat", "layer"),
            P(),
            P(None, ("layer", "feat")),
            P(("layer", "feat")),
            P(None, ("layer", "feat"), None),
        ),
        check_vma=False,
    )
```

profile of v0, /device:TPU:1, one launch (start us, length us, event | category | flops | bytes accessed | tf_op | source)
XLA Modules:
  0.0 725.6 jit_solution(8421036581591228015)
XLA Ops:
  7.2 0.0 all-gather.6.cloned.1.call-start
  7.2 1.5 collective-permute-start
  8.7 1.1 collective-permute-done
  9.7 0.8 broadcast_select_fusion.5
  10.5 3.8 collective-permute-start.1
  14.3 2.1 collective-permute-done.1
  16.5 1.4 collective-permute-start.2
  17.9 2.8 collective-permute-done.2
  20.7 0.7 pad_maximum_fusion
  21.5 0.0 all-gather.6.cloned.1.call-update
  21.5 0.0 copy-start.4
  21.5 0.0 all-reduce.2.cloned.1.call-start
  21.5 52.6 %all-gather.6.cloned.1.call-done = bf16[512,2048]{1,0:T(8,128)(2,1)} async-done(((bf16[64,2048]{1,0:T(8,128)(2,1)}), bf16[512,2048]{1,0:T(8,128)(2,1)}) %all-gather.6.cloned.1.call-update) | async-done | bytes 2097168 | tf_op jit(solution)/shard_map/all_gather | solution.py:48
  74.2 5.1 fusion.7
  79.3 0.0 copy-start.5
  79.3 1.3 copy-done.5
  80.7 0.0 copy-done.4
  80.7 9.4 %convolution_convert_fusion = bf16[512,2,2048]{2,0,1:T(8,128)(2,1)} fusion(bf16[2,1024,2048]{2,1,0:T(8,128)(2,1)} %param.9, f32[512,1024]{1,0:T(8,128)S(1)} %fusion.7, f32[1024]{0:T(1024)S(1)} %copy-done.4), kind=kOutput, calls=%fused_computation.1 | convolution fusion | flops 4298637312 | bytes 14684160 | tf_op jit(solution)/shard_map/tf,kfd->tkd/dot_general | solution.py:51
  90.1 0.0 all-reduce.2.cloned.1.call-update
  90.1 0.0 all-gather.8.cloned.1.call-start
  90.2 184.6 %all-reduce.2.cloned.1.call-done = bf16[512,2,2048]{2,0,1:T(8,128)(2,1)} async-done(((bf16[512,2,2048]{2,0,1:T(8,128)(2,1)}), bf16[512,2,2048]{2,0,1:T(8,128)(2,1)}) %all-reduce.2.cloned.1.call-update) | async-done | bytes 4194320 | tf_op jit(solution)/shard_map/psum | solution.py:54
  274.8 1.9 convert_convert_fusion
  276.7 0.0 all-gather.8.cloned.1.call-update
  276.7 0.0 all-gather.10.cloned.1.call-start
  276.8 0.0 copy-start.2
  276.9 75.4 %all-gather.8.cloned.1.call-done = bf16[1024,2,2048]{2,0,1:T(8,128)(2,1)} async-done(((bf16[64,2,2048]{2,0,1:T(8,128)(2,1)}), bf16[1024,2,2048]{2,0,1:T(8,128)(2,1)}) %all-gather.8.cloned.1.call-update) | async-done | bytes 8388624 | tf_op jit(solution)/shard_map/all_gather | solution.py:56
  352.2 11.3 %bitcast_convert_fusion = f32[16,64,2,2048]{3,1,0,2:T(8,128)} fusion(bf16[1024,2,2048]{2,0,1:T(8,128)(2,1)} %all-gather.8.cloned.1.call-done), kind=kLoop, calls=%fused_computation.30 | loop fusion | flops 4194304 | bytes 25165824 | tf_op jit(solution)/shard_map/convert_element_type | solution.py:58
  363.5 1.7 dynamic-slice_reduce_fusion
  365.2 0.0 copy-done.2
  365.2 0.6 multiply_convert_fusion
  365.9 0.0 copy-start.1
  365.9 0.0 all-gather.10.cloned.1.call-update
  365.9 0.6 multiply_reduce_fusion
  366.5 64.1 %psum.15 = f32[]{:T(128)} all-reduce(f32[]{:T(128)} %multiply_reduce_fusion), channel_id=1, replica_groups=mesh['layer'=16,'feat'=8] {'layer','feat'}, use_global_device_ids=true, to_apply=%region_4.5 | all-reduce | flops 1 | bytes 8 | tf_op jit(solution)/shard_map/psum | solution.py:71
  431.3 238.1 %all-gather.10.cloned.1.call-done = bf16[8192,256]{1,0:T(8,128)(2,1)} async-done(((bf16[64,256]{1,0:T(8,128)(2,1)}), bf16[8192,256]{1,0:T(8,128)(2,1)}) %all-gather.10.cloned.1.call-update) | async-done | bytes 4194320 | tf_op jit(solution)/shard_map/all_gather | solution.py:74
  669.4 2.7 constant_dynamic-slice_fusion
  672.1 0.0 copy-done.1
  672.1 4.4 fusion
  676.5 2.9 stack_reshape.3
  679.4 1.5 constant_dynamic-update-slice_fusion.1
  680.8 3.1 select_n.126
  683.9 0.0 slice-start
  683.9 1.5 constant_dynamic-update-slice_fusion
  685.3 0.0 copy-start
  685.3 0.0 slice-start.1
  685.4 0.0 copy-start.6
  685.4 11.2 %convert_bitcast_fusion = bf16[2,1024,2048]{1,2,0:T(8,128)(2,1)} fusion(bf16[2,512,2048]{2,1,0:T(8,128)(2,1)} %constant_dynamic-update-slice_fusion, f32[512,1024]{1,0:T(8,128)} %copy-done.5, f32[1024]{0:T(1024)S(1)} %copy-done.4), kind=kOutput, calls=%fused_computation | convolution fusion | flops 4300734464 | bytes 14684160 | tf_op jit(solution)/shard_map/tf,ktd->kfd/dot_general | solution.py:84
  696.6 0.0 slice-done
  696.6 0.0 copy-done
  696.6 0.0 slice-done.1
  696.6 0.0 copy-done.6
  696.6 5.2 convert_reduce_fusion
  701.8 0.0 copy-start.3
  701.8 11.7 %copy.13 = bf16[2,1024,2048]{2,1,0:T(8,128)(2,1)} copy(bf16[2,1024,2048]{1,2,0:T(8,128)(2,1)} %convert_bitcast_fusion) | data formatting | bytes 16777216
  713.6 0.0 copy-done.3
  713.6 4.4 convolution_convert_fusion.1
  (5 shorter events, 0.1 us)
Async XLA Ops:
  7.2 67.0 %all-gather.6.cloned.1.call-start = ((), (), s32[]{:S(2)}) async-start(), calls=%async_computation | async-start | bytes 2359296 | tf_op jit(solution)/shard_map/all_gather | solution.py:48
  7.2 2.5 collective-permute-start
  10.5 5.9 collective-permute-start.1
  16.5 4.2 collective-permute-start.2
  21.5 59.2 %copy-start.4 = (f32[1024]{0:T(1024)S(1)}, f32[1024]{0:T(1024)}, u32[]{:S(2)}) copy-start(f32[1024]{0:T(1024)} %param.8) | copy-start | bytes 12292
  21.5 253.3 %all-reduce.2.cloned.1.call-start = ((), (), s32[]{:S(2)}) async-start(), calls=%async_computation.1 | async-start | bytes 8388608 | tf_op jit(solution)/shard_map/psum | solution.py:54
  79.3 1.3 copy-start.5
  90.1 262.1 %all-gather.8.cloned.1.call-start = ((), (), s32[]{:S(2)}) async-start(), calls=%async_computation.2 | async-start | bytes 8912896 | tf_op jit(solution)/shard_map/all_gather | solution.py:56
  276.7 392.6 %all-gather.10.cloned.1.call-start = ((), (), s32[]{:S(2)}) async-start(), calls=%async_computation.3 | async-start | bytes 4227072 | tf_op jit(solution)/shard_map/all_gather | solution.py:74
  276.8 88.4 %copy-start.2 = (bf16[64,256]{1,0:T(8,128)(2,1)S(1)}, bf16[64,256]{1,0:T(8,128)(2,1)}, u32[]{:S(2)}) copy-start(bf16[64,256]{1,0:T(8,128)(2,1)} %param.6) | copy-start | bytes 98308
  365.9 306.2 %copy-start.1 = (f32[64,256]{1,0:T(8,128)}, f32[64,256]{1,0:T(8,128)S(1)}, u32[]{:S(2)}) copy-start(f32[64,256]{1,0:T(8,128)S(1)} %get-tuple-element.13) | copy-start | bytes 196612
  683.9 12.7 %slice-start = ((s8[8388608]{0:T(1024)(128)(4,1)}), s8[4194304]{0:T(1024)(128)(4,1)S(1)}, s32[]{:S(2)}) async-start(s8[8388608]{0:T(1024)(128)(4,1)} %bitcast.31), calls=%async_computation.4 | async-start | bytes 8388608
  685.3 11.2 %copy-start = (bf16[2,512,2048]{2,1,0:T(8,128)(2,1)S(1)}, bf16[2,512,2048]{2,1,0:T(8,128)(2,1)}, u32[]{:S(2)}) copy-start(bf16[2,512,2048]{2,1,0:T(8,128)(2,1)} %constant_dynamic-update-slice_fusion) | copy-start | bytes 12582916
  685.3 11.2 %slice-start.1 = ((s8[8388608]{0:T(1024)(128)(4,1)}), s8[4194304]{0:T(1024)(128)(4,1)S(1)}, s32[]{:S(2)}) async-start(s8[8388608]{0:T(1024)(128)(4,1)} %bitcast.31), calls=%async_computation.5 | async-start | bytes 8388608
  685.4 11.2 %copy-start.6 = (f32[512,1024]{1,0:T(8,128)S(1)}, f32[512,1024]{1,0:T(8,128)}, u32[]{:S(2)}) copy-start(f32[512,1024]{1,0:T(8,128)} %copy-done.5) | copy-start | bytes 6291460
  701.8 11.7 %copy-start.3 = (bf16[512,2048]{1,0:T(8,128)(2,1)S(1)}, bf16[512,2048]{1,0:T(8,128)(2,1)}, u32[]{:S(2)}) copy-start(bf16[512,2048]{1,0:T(8,128)(2,1)} %all-gather.6.cloned.1.call-done) | copy-start | bytes 6291460
Sparse Core Ops, SparseCore 0:
  21.6 52.5 all-gather.5
  90.3 184.5 all-reduce.1
  277.9 74.3 all-gather.7
  366.0 303.3 all-gather.9
where the time goes:
time: 726 us
  waiting for transfers between devices  557 us (77%)
  blocking collectives  64.1 us (9%)
  matrix products  35.4 us (5%)
  local copies, waits for them, and re-layouts  24.7 us (3%)
  other arithmetic  22 us (3%)
  between operations  15.7 us (2%)
    all_gather x1, waiting for transfers between devices, on_device(): lax.all_gather(scaled[None], ('layer', 'feat'), axis=0, tiled=True)  238 us
    psum x1, waiting for transfers between devices, on_device(): lax.psum(partial_value.astype(jnp.bfloat16), 'feat').astype(jnp.float32)  185 us
    all_gather x1, waiting for transfers between devices, on_device(): lax.all_gather(summed_rows[None].astype(jnp.bfloat16), 'layer', axis=0, t...  75.4 us
    psum x1, blocking collectives, on_device(): squares = lax.psum(jnp.sum(recon_error * recon_error), ('layer', 'feat'))  64.1 us
    all_gather x1, waiting for transfers between devices, on_device(): inputs = lax.all_gather(joined, 'feat', axis=0, tiled=True)  52.6 us
    unnamed x20, local copies, waits for them, and re-layouts  14.6 us
  transfers between devices with their start and end apart: 7, of which 7 were waited for; matrix products, arithmetic and copies ran while one was open for 0% of the time, Pallas kernels for 0%

commit v1 on v0

--- a/solution.py
+++ b/solution.py
@@ -71,7 +71,12 @@
     squares = lax.psum(jnp.sum(recon_error * recon_error), ("layer", "feat"))
     mean_square = squares / (LAYERS * TOK * D)
     scaled = (loss_scale / TOK * recon_error).astype(jnp.bfloat16)
-    gathered = lax.all_gather(scaled[None], ("layer", "feat"), axis=0, tiled=True)
+    gathered = jnp.concatenate(
+        lax.all_to_all(
+            jnp.stack([scaled[None]] * lax.axis_size(("layer", "feat"))), ("layer", "feat"), 0, 0
+        ),
+        axis=0,
+    )
     own_grad = arrange_group(gathered, layer_group, feat_count, sub_count)
     next_index = jnp.minimum(layer_group + 1, LAYERS - 1)
     next_grad = arrange_group(gathered, next_index, feat_count, sub_count)

time: 726 us -> 540 us (0.74)
  waiting for transfers between devices: 557 us -> 319 us
  blocking collectives: 64.1 us -> 105 us
  local copies, waits for them, and re-layouts: 24.7 us -> 32.5 us
    all_gather x1 -> x0, waiting for transfers between devices: 238 us -> none  [on_device(): lax.all_gather(scaled[None], ('layer', 'feat'), axis=0, tiled=True)]
    psum x1, blocking collectives: 64.1 us -> 105 us  [on_device(): squares = lax.psum(jnp.sum(recon_error * recon_error), ('layer', 'feat'))]
  transfers between devices with their start and end apart: 7 -> 7, of which waited for: 7 -> 6; matrix products, arithmetic and copies ran while one was open for 0% -> 0% of each run, Pallas kernels for 0% -> 0%
where the time goes in v1:
time: 540 us; the launch traced here: 539 us
  waiting for transfers between devices  319 us (59%)
  blocking collectives  105 us (19%)
  matrix products  35.4 us (7%)
  local copies, waits for them, and re-layouts  32.5 us (6%)
  other arithmetic  19.6 us (4%)
  between operations  15.7 us (3%)
  starting transfers between devices  12.7 us (2%)
    psum x1, waiting for transfers between devices, on_device(): lax.psum(partial_value.astype(jnp.bfloat16), 'feat').astype(jnp.float32)  185 us
    psum x1, blocking collectives, on_device(): squares = lax.psum(jnp.sum(recon_error * recon_error), ('layer', 'feat'))  105 us
    all_gather x1, waiting for transfers between devices, on_device(): lax.all_gather(summed_rows[None].astype(jnp.bfloat16), 'layer', axis=0, t...  75.4 us
    all_gather x1, waiting for transfers between devices, on_device(): inputs = lax.all_gather(joined, 'feat', axis=0, tiled=True)  52.6 us
    unnamed x20, local copies, waits for them, and re-layouts  16.3 us
    convert_element_type x1, other arithmetic, on_device(): gathered = lax.all_gather(summed_rows[None].astype(jnp.bfloat16), 'layer'...  11.3 us
    dot_general x1, matrix products, on_device(): jnp.einsum('tf,ktd->kfd', features, recon_grads, preferred_element_type=j...  11.2 us
  transfers between devices with their start and end apart: 7, of which 6 were waited for; matrix products, arithmetic and copies ran while one was open for 0% of the time, Pallas kernels for 0%

profile of v1, /device:TPU:1, one launch (start us, length us, event | category | flops | bytes accessed | tf_op | source)
XLA Modules:
  0.0 539.3 jit_solution(2553826560692465514)
XLA Ops:
  7.2 0.0 all-gather.4.cloned.1.call-start
  7.2 1.5 collective-permute-start
  8.7 1.1 collective-permute-done
  9.7 0.8 broadcast_select_fusion.5
  10.5 3.8 collective-permute-start.1
  14.3 2.1 collective-permute-done.1
  16.5 1.4 collective-permute-start.2
  17.9 2.8 collective-permute-done.2
  20.7 0.7 pad_maximum_fusion
  21.5 0.0 all-gather.4.cloned.1.call-update
  21.5 0.0 copy-start.4
  21.5 0.0 all-reduce.2.cloned.1.call-start
  21.5 52.6 %all-gather.4.cloned.1.call-done = bf16[512,2048]{1,0:T(8,128)(2,1)} async-done(((bf16[64,2048]{1,0:T(8,128)(2,1)}), bf16[512,2048]{1,0:T(8,128)(2,1)}) %all-gather.4.cloned.1.call-update) | async-done | bytes 2097168 | tf_op jit(solution)/shard_map/all_gather | solution.py:48
  74.2 5.1 fusion.6
  79.3 0.0 copy-start.5
  79.3 1.3 copy-done.5
  80.7 0.0 copy-done.4
  80.7 9.4 %convolution_convert_fusion = bf16[512,2,2048]{2,0,1:T(8,128)(2,1)} fusion(bf16[2,1024,2048]{2,1,0:T(8,128)(2,1)} %param.9, f32[512,1024]{1,0:T(8,128)S(1)} %fusion.6, f32[1024]{0:T(1024)S(1)} %copy-done.4), kind=kOutput, calls=%fused_computation.1 | convolution fusion | flops 4298637312 | bytes 14684160 | tf_op jit(solution)/shard_map/tf,kfd->tkd/dot_general | solution.py:51
  90.1 0.0 all-reduce.2.cloned.1.call-update
  90.1 0.0 all-gather.6.cloned.1.call-start
  90.2 184.6 %all-reduce.2.cloned.1.call-done = bf16[512,2,2048]{2,0,1:T(8,128)(2,1)} async-done(((bf16[512,2,2048]{2,0,1:T(8,128)(2,1)}), bf16[512,2,2048]{2,0,1:T(8,128)(2,1)}) %all-reduce.2.cloned.1.call-update) | async-done | bytes 4194320 | tf_op jit(solution)/shard_map/psum | solution.py:54
  274.8 1.9 convert_convert_fusion
  276.7 0.0 all-gather.6.cloned.1.call-update
  276.8 0.0 copy-start.2
  276.8 75.4 %all-gather.6.cloned.1.call-done = bf16[1024,2,2048]{2,0,1:T(8,128)(2,1)} async-done(((bf16[64,2,2048]{2,0,1:T(8,128)(2,1)}), bf16[1024,2,2048]{2,0,1:T(8,128)(2,1)}) %all-gather.6.cloned.1.call-update) | async-done | bytes 8388624 | tf_op jit(solution)/shard_map/all_gather | solution.py:56
  352.2 11.3 %bitcast_convert_fusion = f32[16,64,2,2048]{3,1,0,2:T(8,128)} fusion(bf16[1024,2,2048]{2,0,1:T(8,128)(2,1)} %all-gather.6.cloned.1.call-done), kind=kLoop, calls=%fused_computation.27 | loop fusion | flops 4194304 | bytes 25165824 | tf_op jit(solution)/shard_map/convert_element_type | solution.py:58
  363.5 1.7 dynamic-slice_reduce_fusion
  365.2 0.0 copy-done.2
  365.2 0.0 copy-start.1
  365.3 2.5 stack.7
  367.8 5.9 %all-to-all-start = ((bf16[128,1,64,256]{3,2,1,0:T(8,128)(2,1)}), bf16[128,1,64,256]{3,2,1,0:T(8,128)(2,1)}, u32[]{:S(2)}, u32[]{:S(2)}) async-start(bf16[128,1,64,256]{3,2,1,0:T(8,128)(2,1)} %stack.7), calls=%async_computation | async-start | bytes 8388608 | tf_op jit(solution)/shard_map/all_to_all | solution.py:75
  373.7 0.0 copy-done.1
  373.8 0.6 multiply_reduce_fusion
  374.4 104.6 %psum.15 = f32[]{:T(128)} all-reduce(f32[]{:T(128)} %multiply_reduce_fusion), channel_id=1, replica_groups=mesh['layer'=16,'feat'=8] {'layer','feat'}, use_global_device_ids=true, to_apply=%region_4.5 | all-reduce | flops 1 | bytes 8 | tf_op jit(solution)/shard_map/psum | solution.py:71
  479.6 0.0 all-to-all-done
  479.6 2.5 select_bitcast_fusion
  482.1 2.6 copy.16
  484.7 4.2 stack_reshape.3
  488.9 3.2 constant_dynamic-update-slice_fusion.1
  492.1 2.6 copy.17
  494.7 2.9 select_n.126
  497.5 0.0 slice-start
  497.5 1.5 constant_dynamic-update-slice_fusion
  499.0 0.0 copy-start
  499.0 0.0 slice-start.1
  499.0 0.0 copy-start.6
  499.0 11.2 %convert_bitcast_fusion = bf16[2,1024,2048]{1,2,0:T(8,128)(2,1)} fusion(bf16[2,512,2048]{2,1,0:T(8,128)(2,1)} %constant_dynamic-update-slice_fusion, f32[512,1024]{1,0:T(8,128)} %copy-done.5, f32[1024]{0:T(1024)S(1)} %copy-done.4), kind=kOutput, calls=%fused_computation | convolution fusion | flops 4300734464 | bytes 14684160 | tf_op jit(solution)/shard_map/tf,ktd->kfd/dot_general | solution.py:89
  510.2 0.0 slice-done
  510.2 0.0 copy-done
  510.2 0.0 slice-done.1
  510.2 0.0 copy-done.6
  510.2 5.2 convert_reduce_fusion
  515.5 0.0 copy-start.3
  515.5 11.7 %copy.19 = bf16[2,1024,2048]{2,1,0:T(8,128)(2,1)} copy(bf16[2,1024,2048]{1,2,0:T(8,128)(2,1)} %convert_bitcast_fusion) | data formatting | bytes 16777216
  527.2 0.0 copy-done.3
  527.2 4.4 convolution_convert_fusion.1
  (6 shorter events, 0.1 us)
Async XLA Ops:
  7.2 67.0 %all-gather.4.cloned.1.call-start = ((), (), s32[]{:S(2)}) async-start(), calls=%async_computation.1 | async-start | bytes 2359296 | tf_op jit(solution)/shard_map/all_gather | solution.py:48
  7.2 2.5 collective-permute-start
  10.5 5.9 %collective-permute-start.1 = (bf16[64,512]{1,0:T(8,128)(2,1)S(1)}, bf16[64,512]{1,0:T(8,128)(2,1)S(1)}, u32[]{:S(2)}, u32[]{:S(2)}) collective-permute-start(bf16[64,512]{1,0:T(8,128)(2,1)S(1)} %pad_maximum_fusion.2), channel_id=1, source_target_pairs={{0,16},{8,24},{16,0},{24,8},{32,48},{40,56},{48,32},{56,40},{64,80... | collective-permute-start | bytes 196616 | tf_op jit(solution)/shard_map/ppermute | solution.py:15
  16.5 4.2 collective-permute-start.2
  21.5 59.2 %copy-start.4 = (f32[1024]{0:T(1024)S(1)}, f32[1024]{0:T(1024)}, u32[]{:S(2)}) copy-start(f32[1024]{0:T(1024)} %param.8) | copy-start | bytes 12292
  21.5 253.3 %all-reduce.2.cloned.1.call-start = ((), (), s32[]{:S(2)}) async-start(), calls=%async_computation.2 | async-start | bytes 8388608 | tf_op jit(solution)/shard_map/psum | solution.py:54
  79.3 1.3 copy-start.5
  90.1 262.1 %all-gather.6.cloned.1.call-start = ((), (), s32[]{:S(2)}) async-start(), calls=%async_computation.3 | async-start | bytes 8912896 | tf_op jit(solution)/shard_map/all_gather | solution.py:56
  276.8 88.4 %copy-start.2 = (bf16[64,256]{1,0:T(8,128)(2,1)S(1)}, bf16[64,256]{1,0:T(8,128)(2,1)}, u32[]{:S(2)}) copy-start(bf16[64,256]{1,0:T(8,128)(2,1)} %param.6) | copy-start | bytes 98308
  365.2 8.5 %copy-start.1 = (f32[64,256]{1,0:T(8,128)}, f32[64,256]{1,0:T(8,128)S(1)}, u32[]{:S(2)}) copy-start(f32[64,256]{1,0:T(8,128)S(1)} %get-tuple-element.23) | copy-start | bytes 196612
  367.8 111.8 %all-to-all-start = ((bf16[128,1,64,256]{3,2,1,0:T(8,128)(2,1)}), bf16[128,1,64,256]{3,2,1,0:T(8,128)(2,1)}, u32[]{:S(2)}, u32[]{:S(2)}) async-start(bf16[128,1,64,256]{3,2,1,0:T(8,128)(2,1)} %stack.7), calls=%async_computation | async-start | bytes 8388608 | tf_op jit(solution)/shard_map/all_to_all | solution.py:75
  497.5 12.7 %slice-start = ((s8[8388608]{0:T(1024)(128)(4,1)}), s8[4194304]{0:T(1024)(128)(4,1)S(1)}, s32[]{:S(2)}) async-start(s8[8388608]{0:T(1024)(128)(4,1)} %bitcast.30), calls=%async_computation.4 | async-start | bytes 8388608
  499.0 11.2 %copy-start = (bf16[2,512,2048]{2,1,0:T(8,128)(2,1)S(1)}, bf16[2,512,2048]{2,1,0:T(8,128)(2,1)}, u32[]{:S(2)}) copy-start(bf16[2,512,2048]{2,1,0:T(8,128)(2,1)} %constant_dynamic-update-slice_fusion) | copy-start | bytes 12582916
  499.0 11.2 %slice-start.1 = ((s8[8388608]{0:T(1024)(128)(4,1)}), s8[4194304]{0:T(1024)(128)(4,1)S(1)}, s32[]{:S(2)}) async-start(s8[8388608]{0:T(1024)(128)(4,1)} %bitcast.30), calls=%async_computation.5 | async-start | bytes 8388608
  499.0 11.2 %copy-start.6 = (f32[512,1024]{1,0:T(8,128)S(1)}, f32[512,1024]{1,0:T(8,128)}, u32[]{:S(2)}) copy-start(f32[512,1024]{1,0:T(8,128)} %copy-done.5) | copy-start | bytes 6291460
  515.5 11.7 %copy-start.3 = (bf16[512,2048]{1,0:T(8,128)(2,1)S(1)}, bf16[512,2048]{1,0:T(8,128)(2,1)}, u32[]{:S(2)}) copy-start(bf16[512,2048]{1,0:T(8,128)(2,1)} %all-gather.4.cloned.1.call-done) | copy-start | bytes 6291460
Sparse Core Ops, SparseCore 0:
  21.6 52.5 all-gather.3
  90.2 184.5 all-reduce.1
  277.9 74.3 all-gather.5
